TPU v7x, 512 devices: a whole 4x8x8 slice. The times are simulated.
512 devices in a mesh: section: 4 (over x), frame: 16 (over y_lo, z), chan: 8 (over y_hi, core).
Axes of the slice: x: 4, y: 8 (y_hi: 4, y_lo: 2; y = y_hi * 2 + y_lo), z: 8, core: 2. Of those that a mesh axis runs over, the one named last changes fastest.
Arguments:
- upstream: bfloat16 [512, 8, 16, 128], P('chan', None, 'frame'), may hold values from -6 to 6
- acts: bfloat16 [4, 512, 8, 16, 128], P('section', None, None, 'frame'), may hold values from -6 to 6
- weights: bfloat16 [4, 27, 512, 512], P('section', None, 'chan'), may hold values from -0.0625 to 0.0625
Outputs:
- grads: bfloat16 [4, 512, 8, 16, 128], P('section', 'chan', None, 'frame')
- weight_grads: bfloat16 [4, 27, 512, 512], P('section', None, 'chan')
All inputs are finite; a program needn't handle non-finite values.
Results may differ from a plain program's by a relative error of at most 0.03.
Values may be sent and summed in bfloat16 or wider, within the bound.
A program may use at most 64 MiB of HBM per device.

v0:
```python
import jax
import jax.numpy as jnp
from jax import lax
from jax.sharding import PartitionSpec as P

BLOCK_FRAMES = 2


def with_halo(cells, sides, width):
    for axis, dim in sides:
        count = lax.axis_size(axis)
        ends = count - 1
        head = lax.slice_in_dim(cells, 0, width, axis=dim)
        tail = lax.slice_in_dim(cells, cells.shape[dim] - width, cells.shape[dim], axis=dim)
        cells = jnp.concatenate(
            [
                lax.ppermute(tail, axis, [(i, (i + 1) % count) for i in range(ends)]),
                cells,
                lax.ppermute(head, axis, [((i + 1) % count, i) for i in range(ends)]),
            ],
            axis=dim,
        )
    return cells


def shifted(value, axis, steps):
    count = lax.axis_size(axis)
    leading, last = (max(0, -steps), min(count, count - steps))
    return lax.ppermute(value, axis, [(source, source + steps) for source in range(leading, last)])


def derivative(stored):
    logistic = jax.nn.sigmoid(stored)
    return logistic * (1.0 + stored * (1.0 - logistic))


def tap_matrix(extended, frames_n, rows_n, width_n):
    pieces = []
    for t_lag in range(3):
        for r_off in (-1, 0, 1):
            for w_off in (-1, 0, 1):
                pieces.append(
                    extended[
                        :,
                        t_lag : t_lag + frames_n,
                        1 - r_off : 1 - r_off + rows_n,
                        1 - w_off : 1 - w_off + width_n,
                    ]
                )
    stacked = jnp.stack(pieces, axis=0)
    return stacked.reshape(stacked.shape[0] * stacked.shape[1], -1)


def body(upstream, acts, weights):
    group = upstream.shape[0]
    frames_all = upstream.shape[1]
    rows_n = upstream.shape[2]
    width_n = upstream.shape[3]
    channels = acts.shape[1]
    blocks_n = frames_all // BLOCK_FRAMES
    cells = BLOCK_FRAMES * rows_n * width_n
    sections = lax.axis_size("section")
    section_pos = lax.axis_index("section")
    chan_pos = lax.axis_index("chan")
    kernel_mat = weights[0].reshape(27 * group, channels)
    stored_all = acts[0]
    later = jnp.zeros((group, 2, rows_n + 2, width_n), jnp.bfloat16)
    inbound = jnp.zeros((group, BLOCK_FRAMES, rows_n, width_n), jnp.bfloat16)
    results = jnp.zeros((group, frames_all, rows_n, width_n), jnp.bfloat16)
    kernel_sum = jnp.zeros((27 * group, channels), jnp.float32)
    ticks = blocks_n + sections - 1
    for tick in range(ticks):
        order = tick - section_pos
        active = jnp.logical_and(order >= 0, order < blocks_n)
        first = (blocks_n - 1 - jnp.clip(order, 0, blocks_n - 1)) * BLOCK_FRAMES
        fresh = lax.dynamic_slice_in_dim(upstream, first, BLOCK_FRAMES, 1)
        current = jnp.where(section_pos == 0, fresh, inbound)
        framed = with_halo(current, (("frame", 2),), 1)
        extended = jnp.pad(
            jnp.concatenate([framed, later], axis=1), ((0, 0), (0, 0), (0, 0), (1, 1))
        )
        taps_mat = tap_matrix(extended, BLOCK_FRAMES, rows_n, width_n)
        stored = lax.dynamic_slice_in_dim(stored_all, first, BLOCK_FRAMES, 1)

        def busy(operand):
            return lax.dot_general(
                kernel_mat, taps_mat, (((0,), (0,)), ((), ())), preferred_element_type=jnp.float32
            )

        def resting(operand):
            return jnp.zeros((group * lax.axis_size("chan"), cells), jnp.float32)

        summed = lax.psum_scatter(
            lax.cond(active, busy, resting, 0).astype(jnp.bfloat16),
            "chan",
            scatter_dimension=0,
            tiled=True,
        ).astype(jnp.float32)
        own = lax.dynamic_slice_in_dim(stored, chan_pos * group, group, 0).astype(jnp.float32)
        updated = (
            current.astype(jnp.float32) + derivative(own) * summed.reshape(current.shape)
        ).astype(jnp.bfloat16)

        def add_kernel(total):
            values = stored.astype(jnp.float32)
            features = (
                (values * jax.nn.sigmoid(values)).astype(jnp.bfloat16).reshape(channels, cells)
            )
            return total + lax.dot_general(
                taps_mat, features, (((1,), (1,)), ((), ())), preferred_element_type=jnp.float32
            )

        def keep_kernel(total):
            return total

        kernel_sum = lax.cond(active, add_kernel, keep_kernel, kernel_sum)
        written = lax.dynamic_update_slice_in_dim(results, updated, first, 1)
        results = jnp.where(active, written, results)
        later = jnp.where(active, framed, later)
        if tick + 1 < ticks:
            inbound = shifted(updated, "section", 1)
    kernel_total = lax.psum(kernel_sum.astype(jnp.bfloat16), "frame")
    return (results[None], kernel_total.reshape(1, 27, group, channels))


def solution(mesh):
    placed = (
        P("chan", None, "frame", None),
        P("section", None, None, "frame", None),
        P("section", None, "chan", None),
    )
    return jax.shard_map(
        body,
        mesh=mesh,
        in_specs=placed,
        out_specs=(P("section", "chan", None, "frame", None), P("section", None, "chan", None)),
        check_vma=False,
    )
```

profile of v0, /device:TPU:2, one launch (start us, length us, event | category | flops | bytes accessed | tf_op | source)
XLA Modules:
  0.0 595.2 jit_solution(7948391413461682318)
XLA Ops:
  8.2 4.3 collective-permute-start
  14.0 4.6 collective-permute-done.1
  23.6 43.8 %reduce-scatter.8.cloned.1.call-done = bf16[64,256]{1,0:T(8,128)(2,1)} async-done(((bf16[512,256]{1,0:T(8,128)(2,1)}), bf16[64,256]{1,0:T(8,128)(2,1)}) %reduce-scatter.8.cloned.1.call-update) | async-done | bytes 32784 | tf_op jit(solution)/shard_map/reduce_scatter | solution.py:93
  74.3 3.5 collective-permute-start.3
  79.4 4.2 collective-permute-done.4
  91.2 36.6 %reduce-scatter.10.cloned.1.call-done = bf16[64,256]{1,0:T(8,128)(2,1)} async-done(((bf16[512,256]{1,0:T(8,128)(2,1)}), bf16[64,256]{1,0:T(8,128)(2,1)}) %reduce-scatter.10.cloned.1.call-update) | async-done | bytes 32784 | tf_op jit(solution)/shard_map/reduce_scatter | solution.py:93
  134.7 3.5 collective-permute-start.6
  139.8 4.2 collective-permute-done.7
  151.3 38.1 %reduce-scatter.12.cloned.1.call-done = bf16[64,256]{1,0:T(8,128)(2,1)} async-done(((bf16[512,256]{1,0:T(8,128)(2,1)}), bf16[64,256]{1,0:T(8,128)(2,1)}) %reduce-scatter.12.cloned.1.call-update) | async-done | bytes 32784 | tf_op jit(solution)/shard_map/reduce_scatter | solution.py:93
  197.6 4.7 collective-permute-start.9
  211.4 39.8 %reduce-scatter.14.cloned.1.call-done = bf16[64,256]{1,0:T(8,128)(2,1)} async-done(((bf16[512,256]{1,0:T(8,128)(2,1)}), bf16[64,256]{1,0:T(8,128)(2,1)}) %reduce-scatter.14.cloned.1.call-update) | async-done | bytes 32784 | tf_op jit(solution)/shard_map/reduce_scatter | solution.py:93
  258.1 3.6 collective-permute-start.12
  263.2 4.2 collective-permute-done.13
  274.7 38.2 %reduce-scatter.16.cloned.1.call-done = bf16[64,256]{1,0:T(8,128)(2,1)} async-done(((bf16[512,256]{1,0:T(8,128)(2,1)}), bf16[64,256]{1,0:T(8,128)(2,1)}) %reduce-scatter.16.cloned.1.call-update) | async-done | bytes 32784 | tf_op jit(solution)/shard_map/reduce_scatter | solution.py:93
  319.8 3.6 collective-permute-start.15
  325.0 4.2 collective-permute-done.16
  334.4 40.5 %reduce-scatter.18.cloned.1.call-done = bf16[64,256]{1,0:T(8,128)(2,1)} async-done(((bf16[512,256]{1,0:T(8,128)(2,1)}), bf16[64,256]{1,0:T(8,128)(2,1)}) %reduce-scatter.18.cloned.1.call-update) | async-done | bytes 32784 | tf_op jit(solution)/shard_map/reduce_scatter | solution.py:93
  386.9 4.2 collective-permute-done.19
  396.4 6.4 %conditional.22 = (f32[1728,512]{1,0:T(8,128)S(1)}) conditional(s32[]{:T(128)} %convert_element_type.269, f32[1728,512]{1,0:T(8,128)S(1)} %get-tuple-element.296, (bf16[1,512,8,1,128]{4,2,3,1,0:T(8,128)(2,1)}, bf16[1728,256]{1,0:T(8,128)(2,1)}, f32[1728,512]{1,0:T(8,128)S(1)}, s32[]{:T(128)}) %tuple.125), branch_computations={%region_23.24_spmd, %region_24.25_spmd.clone} | conditional | flops 454656000 | bytes 11894796 | solution.py:116
  402.8 6.8 %conditional.23 = (f32[1728,512]{1,0:T(8,128)S(1)}) conditional(s32[]{:T(128)} %convert_element_type.275, f32[1728,512]{1,0:T(8,128)S(1)} %get-tuple-element.297, (bf16[1,512,8,1,128]{4,2,3,1,0:T(8,128)(2,1)}, bf16[1728,256]{1,0:T(8,128)(2,1)}, f32[1728,512]{1,0:T(8,128)S(1)}, s32[]{:T(128)}) %tuple.126), branch_computations={%region_25.26_spmd, %region_26.27_spmd.clone} | conditional | flops 454656000 | bytes 11894796 | solution.py:116
  409.6 6.4 %conditional.24 = (f32[1728,512]{1,0:T(8,128)S(1)}) conditional(s32[]{:T(128)} %convert_element_type.281, f32[1728,512]{1,0:T(8,128)S(1)} %get-tuple-element.298, (bf16[1,512,8,1,128]{4,2,3,1,0:T(8,128)(2,1)}, bf16[1728,256]{1,0:T(8,128)(2,1)}, f32[1728,512]{1,0:T(8,128)S(1)}, s32[]{:T(128)}) %tuple.127), branch_computations={%region_27.28_spmd, %region_28.29_spmd.clone} | conditional | flops 454656000 | bytes 11894796 | solution.py:116
  416.0 6.6 %conditional.25 = (f32[1728,512]{1,0:T(8,128)S(1)}) conditional(s32[]{:T(128)} %convert_element_type.287, f32[1728,512]{1,0:T(8,128)S(1)} %get-tuple-element.299, (bf16[1,512,8,1,128]{4,2,3,1,0:T(8,128)(2,1)}, bf16[1728,256]{1,0:T(8,128)(2,1)}, f32[1728,512]{1,0:T(8,128)S(1)}, s32[]{:T(128)}) %tuple.128), branch_computations={%region_29.30_spmd, %region_30.31_spmd.clone} | conditional | flops 454656000 | bytes 11894796 | solution.py:116
  425.2 10.9 %reduce-scatter.20.cloned.1.call-done = bf16[64,256]{1,0:T(8,128)(2,1)} async-done(((bf16[512,256]{1,0:T(8,128)(2,1)}), bf16[64,256]{1,0:T(8,128)(2,1)}) %reduce-scatter.20.cloned.1.call-update) | async-done | bytes 32784 | tf_op jit(solution)/shard_map/reduce_scatter | solution.py:93
  438.1 147.1 %all-reduce.10.cloned.1.call-done = bf16[1,27,64,512]{3,2,1,0:T(8,128)(2,1)} async-done(((bf16[1,27,64,512]{3,2,1,0:T(8,128)(2,1)}), bf16[1,27,64,512]{3,2,1,0:T(8,128)(2,1)}) %all-reduce.10.cloned.1.call-update) | async-done | bytes 1769488 | tf_op jit(solution)/shard_map/psum | solution.py:122
  (336 shorter events, 145.4 us)
Async XLA Ops:
  7.2 60.2 %reduce-scatter.8.cloned.1.call-start = ((), (), s32[]{:S(2)}) async-start(), calls=%async_computation.7 | async-start | bytes 294912 | tf_op jit(solution)/shard_map/reduce_scatter | solution.py:93
  8.2 5.9 collective-permute-start
  12.5 6.2 %collective-permute-start.1 = (bf16[64,2,1,128]{3,1,0,2:T(2,128)(2,1)S(1)}, bf16[64,2,1,128]{3,1,0,2:T(2,128)(2,1)S(1)}, u32[]{:S(2)}, u32[]{:S(2)}) collective-permute-start(bf16[64,2,1,128]{3,1,0,2:T(2,128)(2,1)S(1)} %broadcast_select_fusion.18), channel_id=1, source_target_pairs={{8,0},{16,8},{24,16},{32,24},{40,32},{48,40},{56,48},{64,56},{72,6... | collective-permute-start | bytes 98312 | tf_op jit(solution)/shard_map/ppermute | solution.py:19
  23.5 104.3 %reduce-scatter.10.cloned.1.call-start = ((), (), s32[]{:S(2)}) async-start(), calls=%async_computation.8 | async-start | bytes 294912 | tf_op jit(solution)/shard_map/reduce_scatter | solution.py:93
  68.4 5.8 collective-permute-start.2
  77.9 5.8 collective-permute-start.4
  91.2 98.2 %reduce-scatter.12.cloned.1.call-start = ((), (), s32[]{:S(2)}) async-start(), calls=%async_computation.9 | async-start | bytes 294912 | tf_op jit(solution)/shard_map/reduce_scatter | solution.py:93
  128.8 5.8 collective-permute-start.5
  138.2 5.8 collective-permute-start.7
  151.3 99.9 %reduce-scatter.14.cloned.1.call-start = ((), (), s32[]{:S(2)}) async-start(), calls=%async_computation.10 | async-start | bytes 294912 | tf_op jit(solution)/shard_map/reduce_scatter | solution.py:93
  190.5 5.8 collective-permute-start.8
  196.3 6.0 %collective-permute-start.10 = (bf16[64,2,1,128]{3,1,0,2:T(2,128)(2,1)S(1)}, bf16[64,2,1,128]{3,1,0,2:T(2,128)(2,1)S(1)}, u32[]{:S(2)}, u32[]{:S(2)}) collective-permute-start(bf16[64,2,1,128]{3,1,0,2:T(2,128)(2,1)S(1)} %broadcast_select_fusion.15), channel_id=1, source_target_pairs={{8,0},{16,8},{24,16},{32,24},{40,32},{48,40},{56,48},{64,56},{72,6... | collective-permute-start | bytes 98312 | tf_op jit(solution)/shard_map/ppermute | solution.py:19
  197.6 6.1 %collective-permute-start.9 = (bf16[64,2,1,128]{3,1,0,2:T(2,128)(2,1)S(1)}, bf16[64,2,1,128]{3,1,0,2:T(2,128)(2,1)S(1)}, u32[]{:S(2)}, u32[]{:S(2)}) collective-permute-start(bf16[64,2,1,128]{3,1,0,2:T(2,128)(2,1)S(1)} %broadcast_select_fusion.15), channel_id=1, source_target_pairs={{0,8},{8,16},{16,24},{24,32},{32,40},{40,48},{48,56},{56,64},{64,7... | collective-permute-start | bytes 98312 | tf_op jit(solution)/shard_map/ppermute | solution.py:17
  211.3 101.6 %reduce-scatter.16.cloned.1.call-start = ((), (), s32[]{:S(2)}) async-start(), calls=%async_computation.11 | async-start | bytes 294912 | tf_op jit(solution)/shard_map/reduce_scatter | solution.py:93
  252.2 5.8 collective-permute-start.11
  258.1 5.2 collective-permute-start.12
  261.7 5.8 collective-permute-start.13
  274.6 100.2 %reduce-scatter.18.cloned.1.call-start = ((), (), s32[]{:S(2)}) async-start(), calls=%async_computation.12 | async-start | bytes 294912 | tf_op jit(solution)/shard_map/reduce_scatter | solution.py:93
  313.9 5.8 collective-permute-start.14
  323.4 5.8 collective-permute-start.16
  334.3 101.8 %reduce-scatter.20.cloned.1.call-start = ((), (), s32[]{:S(2)}) async-start(), calls=%async_computation.13 | async-start | bytes 294912 | tf_op jit(solution)/shard_map/reduce_scatter | solution.py:93
  375.9 5.8 collective-permute-start.17
  385.3 5.8 collective-permute-start.19
  395.9 189.4 %all-reduce.10.cloned.1.call-start = ((), (), s32[]{:S(2)}) async-start(), calls=%async_computation.14 | async-start | bytes 3538944 | tf_op jit(solution)/shard_map/psum | solution.py:122
  (17 other events, 311.0 us)
Sparse Core Ops, SparseCore 0:
  23.7 43.6 reduce-scatter.7
  91.3 36.4 reduce-scatter.9
  151.4 38.0 reduce-scatter.11
  211.4 39.6 reduce-scatter.13
  274.7 38.1 reduce-scatter.15
  334.5 40.3 reduce-scatter.17
  396.0 40.0 reduce-scatter.19
  439.9 145.2 all-reduce.9
where the time goes:
time: 605 us; the launch traced here: 595 us
  waiting for transfers between devices  438 us (72%)
  starting transfers between devices  56.5 us (9%)
  local copies, waits for them, and re-layouts  54 us (9%)
  matrix products  17.1 us (3%)
  between operations  15.3 us (3%)
  other arithmetic  13.1 us (2%)
    reduce_scatter x7, waiting for transfers between devices, body(): lax.psum_scatter(lax.cond(active, busy, resting, 0).astype(jnp.bfloat16),...  248 us
    psum x1, waiting for transfers between devices, body(): kernel_total = lax.psum(kernel_sum.astype(jnp.bfloat16), 'frame')  147 us
    unnamed x216, local copies, waits for them, and re-layouts  33.3 us
    ppermute x7, starting transfers between devices, with_halo(): lax.ppermute(tail, axis, [(i, (i + 1) % count) for i in range(ends)])  26.8 us
    ppermute x7, waiting for transfers between devices, with_halo(): lax.ppermute(head, axis, [((i + 1) % count, i) for i in range(ends)])  25.7 us
    ppermute x6, starting transfers between devices, shifted(): lax.ppermute(value, axis, [(source, source + steps) for source in range(l...  20.1 us
    ppermute x6, waiting for transfers between devices, shifted(): lax.ppermute(value, axis, [(source, source + steps) for source in range(l...  14.6 us
    another operation x7, local copies, waits for them, and re-layouts  13.6 us
  transfers between devices with their start and end apart: 28, of which 27 were waited for; matrix products, arithmetic and copies ran while one was open for 5% of the time, Pallas kernels for 0%

commit v1 on v0

--- a/solution.py
+++ b/solution.py
@@ -119,7 +119,9 @@
         later = jnp.where(active, framed, later)
         if tick + 1 < ticks:
             inbound = shifted(updated, "section", 1)
-    kernel_total = lax.psum(kernel_sum.astype(jnp.bfloat16), "frame")
+    block = kernel_sum.astype(jnp.bfloat16)
+    parts = lax.all_gather(block, "frame", axis=0, tiled=False)
+    kernel_total = parts.sum(axis=0)
     return (results[None], kernel_total.reshape(1, 27, group, channels))
 
 

time: 605 us -> 771 us (1.27)
  the two profiles are of different devices: /device:TPU:2 before, /device:TPU:1 now
where the time goes in v1:
time: 771 us; the launch traced here: 761 us
  waiting for transfers between devices  591 us (77%)
  starting transfers between devices  57.7 us (7%)
  local copies, waits for them, and re-layouts  49.5 us (6%)
  other arithmetic  24.7 us (3%)
  matrix products  16.9 us (2%)
  between operations  15.3 us (2%)
    all_gather x1, waiting for transfers between devices, body(): parts = lax.all_gather(block, 'frame', axis=0, tiled=False)  305 us
    reduce_scatter x7, waiting for transfers between devices, body(): lax.psum_scatter(lax.cond(active, busy, resting, 0).astype(jnp.bfloat16),...  273 us
    unnamed x215, local copies, waits for them, and re-layouts  30.5 us
    ppermute x7, starting transfers between devices, with_halo(): lax.ppermute(tail, axis, [(i, (i + 1) % count) for i in range(ends)])  29.8 us
    ppermute x6, starting transfers between devices, shifted(): lax.ppermute(value, axis, [(source, source + steps) for source in range(l...  18.5 us
  transfers between devices with their start and end apart: 28, of which 21 were waited for; matrix products, arithmetic and copies ran while one was open for 4% of the time, Pallas kernels for 0%

profile of v1, /device:TPU:1, one launch (start us, length us, event | category | flops | bytes accessed | tf_op | source)
XLA Modules:
  0.0 761.0 jit_solution(8189631263631125123)
XLA Ops:
  9.5 5.5 collective-permute-start
  23.1 43.9 %reduce-scatter.8.cloned.1.call-done = bf16[64,256]{1,0:T(8,128)(2,1)} async-done(((bf16[512,256]{1,0:T(8,128)(2,1)}), bf16[64,256]{1,0:T(8,128)(2,1)}) %reduce-scatter.8.cloned.1.call-update) | async-done | bytes 32784 | tf_op jit(solution)/shard_map/reduce_scatter | solution.py:93
  73.5 4.0 collective-permute-start.3
  86.0 41.3 %reduce-scatter.10.cloned.1.call-done = bf16[64,256]{1,0:T(8,128)(2,1)} async-done(((bf16[512,256]{1,0:T(8,128)(2,1)}), bf16[64,256]{1,0:T(8,128)(2,1)}) %reduce-scatter.10.cloned.1.call-update) | async-done | bytes 32784 | tf_op jit(solution)/shard_map/reduce_scatter | solution.py:93
  133.8 4.0 collective-permute-start.6
  146.1 42.8 %reduce-scatter.12.cloned.1.call-done = bf16[64,256]{1,0:T(8,128)(2,1)} async-done(((bf16[512,256]{1,0:T(8,128)(2,1)}), bf16[64,256]{1,0:T(8,128)(2,1)}) %reduce-scatter.12.cloned.1.call-update) | async-done | bytes 32784 | tf_op jit(solution)/shard_map/reduce_scatter | solution.py:93
  195.3 4.2 collective-permute-start.9
  207.9 42.7 %reduce-scatter.14.cloned.1.call-done = bf16[64,256]{1,0:T(8,128)(2,1)} async-done(((bf16[512,256]{1,0:T(8,128)(2,1)}), bf16[64,256]{1,0:T(8,128)(2,1)}) %reduce-scatter.14.cloned.1.call-update) | async-done | bytes 32784 | tf_op jit(solution)/shard_map/reduce_scatter | solution.py:93
  257.1 4.1 collective-permute-start.12
  267.0 45.0 %reduce-scatter.16.cloned.1.call-done = bf16[64,256]{1,0:T(8,128)(2,1)} async-done(((bf16[512,256]{1,0:T(8,128)(2,1)}), bf16[64,256]{1,0:T(8,128)(2,1)}) %reduce-scatter.16.cloned.1.call-update) | async-done | bytes 32784 | tf_op jit(solution)/shard_map/reduce_scatter | solution.py:93
  318.4 4.0 collective-permute-start.15
  328.6 45.0 %reduce-scatter.18.cloned.1.call-done = bf16[64,256]{1,0:T(8,128)(2,1)} async-done(((bf16[512,256]{1,0:T(8,128)(2,1)}), bf16[64,256]{1,0:T(8,128)(2,1)}) %reduce-scatter.18.cloned.1.call-update) | async-done | bytes 32784 | tf_op jit(solution)/shard_map/reduce_scatter | solution.py:93
  380.2 4.2 collective-permute-start.18
  390.0 5.1 conditional.21
  395.2 6.4 conditional.22
  395.2 3.4 copy.28
  401.6 6.8 conditional.23
  402.0 3.4 copy.29
  408.4 6.4 conditional.24
  408.4 3.4 copy.30
  415.0 5.0 conditional.27
  422.4 12.4 %reduce-scatter.20.cloned.1.call-done = bf16[64,256]{1,0:T(8,128)(2,1)} async-done(((bf16[512,256]{1,0:T(8,128)(2,1)}), bf16[64,256]{1,0:T(8,128)(2,1)}) %reduce-scatter.20.cloned.1.call-update) | async-done | bytes 32784 | tf_op jit(solution)/shard_map/reduce_scatter | solution.py:93
  436.9 305.4 %all-gather.3.cloned.1.call-done = bf16[27648,512]{1,0:T(8,128)(2,1)} async-done(((bf16[1728,512]{1,0:T(8,128)(2,1)}), bf16[27648,512]{1,0:T(8,128)(2,1)}) %all-gather.3.cloned.1.call-update) | async-done | bytes 28311568 | tf_op jit(solution)/shard_map/all_gather | solution.py:123
  742.3 11.6 %reduce_sum.12 = bf16[1728,512]{1,0:T(8,128)(2,1)} reduce(bf16[16,1728,512]{2,1,0:T(8,128)(2,1)} %bitcast.902, bf16[]{:T(256)} %constant.234.clone.1), dimensions={0}, to_apply=%region_35.36 | reduce | flops 13271040 | bytes 30081026 | tf_op jit(solution)/shard_map/reduce_sum | solution.py:124
  (337 shorter events, 119.5 us)
Async XLA Ops:
  7.2 59.8 %reduce-scatter.8.cloned.1.call-start = ((), (), s32[]{:S(2)}) async-start(), calls=%async_computation.7 | async-start | bytes 294912 | tf_op jit(solution)/shard_map/reduce_scatter | solution.py:93
  8.2 6.8 collective-permute-start.1
  9.5 6.5 collective-permute-start
  23.1 104.2 %reduce-scatter.10.cloned.1.call-start = ((), (), s32[]{:S(2)}) async-start(), calls=%async_computation.8 | async-start | bytes 294912 | tf_op jit(solution)/shard_map/reduce_scatter | solution.py:93
  72.2 5.3 collective-permute-start.4
  73.5 5.0 collective-permute-start.3
  86.0 102.9 %reduce-scatter.12.cloned.1.call-start = ((), (), s32[]{:S(2)}) async-start(), calls=%async_computation.9 | async-start | bytes 294912 | tf_op jit(solution)/shard_map/reduce_scatter | solution.py:93
  128.3 4.1 collective-permute-start.5
  132.5 5.3 collective-permute-start.7
  133.8 5.0 collective-permute-start.6
  146.0 104.6 %reduce-scatter.14.cloned.1.call-start = ((), (), s32[]{:S(2)}) async-start(), calls=%async_computation.10 | async-start | bytes 294912 | tf_op jit(solution)/shard_map/reduce_scatter | solution.py:93
  194.0 5.5 collective-permute-start.10
  195.3 5.0 collective-permute-start.9
  207.8 104.1 %reduce-scatter.16.cloned.1.call-start = ((), (), s32[]{:S(2)}) async-start(), calls=%async_computation.11 | async-start | bytes 294912 | tf_op jit(solution)/shard_map/reduce_scatter | solution.py:93
  255.8 5.4 collective-permute-start.13
  257.1 5.1 collective-permute-start.12
  266.9 106.7 %reduce-scatter.18.cloned.1.call-start = ((), (), s32[]{:S(2)}) async-start(), calls=%async_computation.12 | async-start | bytes 294912 | tf_op jit(solution)/shard_map/reduce_scatter | solution.py:93
  317.1 5.3 collective-permute-start.16
  318.4 5.0 collective-permute-start.15
  328.6 106.3 %reduce-scatter.20.cloned.1.call-start = ((), (), s32[]{:S(2)}) async-start(), calls=%async_computation.13 | async-start | bytes 294912 | tf_op jit(solution)/shard_map/reduce_scatter | solution.py:93
  374.7 4.1 collective-permute-start.17
  378.9 5.5 collective-permute-start.19
  380.2 5.0 collective-permute-start.18
  390.0 352.3 %all-gather.3.cloned.1.call-start = ((), (), s32[]{:S(2)}) async-start(), calls=%async_computation.14 | async-start | bytes 30081024 | tf_op jit(solution)/shard_map/all_gather | solution.py:123
  (18 other events, 475.5 us)
Sparse Core Ops, SparseCore 0:
  23.2 43.7 reduce-scatter.7
  86.1 41.1 reduce-scatter.9
  146.1 42.6 reduce-scatter.11
  208.0 42.5 reduce-scatter.13
  267.1 44.8 reduce-scatter.15
  328.7 44.9 reduce-scatter.17
  390.1 44.7 reduce-scatter.19
  437.7 304.5 all-gather.2
